TPU v7x, 128 devices: a whole 4x4x4 slice. The times are simulated.
128 devices in a mesh: corpus: 16 (over z, y), fsdp: 2 (over core), tensor: 4 (over x).
Axes of the slice: x: 4, y: 4, z: 4, core: 2. Of those that a mesh axis runs over, the one named last changes fastest.
Arguments:
- queries_in: bfloat16 [4096, 4096], P(('corpus', 'fsdp')), may hold values from -6 to 6
- head_weight: bfloat16 [4096, 4096], P('fsdp', 'tensor'), may hold values from -0.09375 to 0.09375
- passages: bfloat16 [16384, 4096], P('corpus', 'tensor'), may hold values from -0.15625 to 0.15625
- teacher: float32 [4096, 4, 32], P(('corpus', 'fsdp')), may hold values from -250 to 400
- cand_block: int32 [4096, 4], P(('corpus', 'fsdp')), may hold values from 0 to 127, all different within a row; in each aligned block of 128 rows (0 to 127, 128 to 255, ...) at most 6 rows name the same one
- cand_offset: int32 [4096, 4, 32], P(('corpus', 'fsdp')), may hold values from 0 to 127, as said below
- block_slot: int32 [128], replicated, may hold values from 0 to 127, each once
Outputs:
- kl_loss: float32 [4096], P(('corpus', 'fsdp'))
- head_grad: float32 [4096, 4096], P('fsdp', 'tensor')
Inputs may be any that keep to these rules, and one draw needn't show every extreme that they name: `cand_block`: in the rows of one device no block id appears more than 6 times, and some block id appears exactly 6 times there; the 4 ids of one query differ. `cand_offset`: the 32 offsets of one query in one block differ. `block_slot`: each storage position is taken by exactly one block.
All inputs are finite; a program needn't handle non-finite values.
Results may differ from a plain program's by a relative error of at most 0.012.
The roundings to bfloat16 on the way count: a program that leaves them out, or rounds other values in their place, can miss the bound.
Values may be sent and summed in bfloat16 or wider, within the bound.
A program may use at most 128 MiB of HBM per device.

v0:
```python
import jax
import jax.numpy as jnp
from jax import lax
from jax.sharding import PartitionSpec as P

ROWS = 128
MOSTB = 6
SWAP = [(0, 1), (1, 0)]


def on_device(queries_in, head_weight, passages, teacher, cand_block, cand_offset, block_slot):
    query_rows, width = queries_in.shape
    half = width // 2
    cols = head_weight.shape[1]
    per_query = cand_block.shape[1]
    offset_count = cand_offset.shape[2]
    total_blocks = block_slot.shape[0]
    n_corpus = lax.axis_size("corpus")
    blocks_here = passages.shape[0] // ROWS
    slot_total = total_blocks * MOSTB
    slots_each = blocks_here * MOSTB
    picks = query_rows * per_query
    first = lax.axis_index("fsdp") == 0
    low, high = (queries_in[:, :half], queries_in[:, half:])
    mine = jnp.where(first, low, high)
    other = jnp.where(first, high, low)
    theirs = lax.ppermute(other, "fsdp", SWAP)
    part_theirs = jnp.dot(theirs, head_weight, preferred_element_type=jnp.float32)
    back = lax.ppermute(part_theirs, "fsdp", SWAP)
    part_mine = jnp.dot(mine, head_weight, preferred_element_type=jnp.float32)
    query = (part_mine + back).astype(jnp.bfloat16)
    all_mine = lax.all_gather(mine, "corpus", axis=0, tiled=True)
    all_theirs = lax.all_gather(theirs, "corpus", axis=0, tiled=True)
    block_ids = lax.broadcasted_iota(jnp.int32, (1, total_blocks), 1)
    named = (cand_block.reshape(-1, 1) == block_ids).astype(jnp.int32)
    slot_of = jnp.sum(named * block_slot.reshape(1, -1), axis=1)
    hits = slot_of[:, None] == block_ids
    before = (
        lax.broadcasted_iota(jnp.int32, (picks, picks), 1)
        < lax.broadcasted_iota(jnp.int32, (picks, picks), 0)
    ).astype(jnp.bfloat16)
    earlier = jnp.dot(before, hits.astype(jnp.bfloat16), preferred_element_type=jnp.float32)
    slot_rank = jnp.sum(jnp.where(hits, earlier, 0.0), axis=1).astype(jnp.int32)
    position = slot_of * MOSTB + slot_rank
    slot_ids = lax.broadcasted_iota(jnp.int32, (slot_total, 1), 0)
    place = (slot_ids == position.reshape(1, -1)).astype(jnp.bfloat16)
    by_query = position.reshape(query_rows, per_query)
    owner = slot_ids == by_query[:, 0].reshape(1, -1)
    for g in range(1, per_query):
        owner = owner | (slot_ids == by_query[:, g].reshape(1, -1))
    owner = owner.astype(jnp.bfloat16)
    slot_block = slot_ids % slots_each // MOSTB
    send_queries = jnp.dot(owner, query, preferred_element_type=jnp.float32).astype(jnp.bfloat16)
    got_queries = lax.all_to_all(
        send_queries.reshape(n_corpus, slots_each, cols), "corpus", 0, 0, tiled=True
    ).reshape(slot_total, cols)
    wide = lax.dot_general(
        got_queries, passages, (((1,), (1,)), ((), ())), preferred_element_type=jnp.float32
    )
    scores = wide[:, :ROWS]
    for j in range(1, blocks_here):
        scores = jnp.where(slot_block == j, wide[:, j * ROWS : (j + 1) * ROWS], scores)
    returned = lax.all_to_all(
        scores.reshape(n_corpus, slots_each, ROWS), "corpus", 0, 0, tiled=True
    ).reshape(slot_total, ROWS)
    picked = returned[position]
    offsets = cand_offset.reshape(picks, offset_count)
    row_ids = lax.broadcasted_iota(jnp.int32, (1, 1, ROWS), 2)
    chosen = offsets[:, :, None] == row_ids
    partial = jnp.sum(jnp.where(chosen, picked[:, None, :], 0.0), axis=2)
    total = partial.reshape(query_rows, per_query * offset_count)
    total = total + lax.ppermute(total, "tensor", [(0, 1), (1, 0), (2, 3), (3, 2)])
    total = total + lax.ppermute(total, "tensor", [(0, 2), (2, 0), (1, 3), (3, 1)])
    student = 50.0 * total
    cached = teacher.reshape(query_rows, per_query * offset_count)
    log_student = student - jax.nn.logsumexp(student, axis=1, keepdims=True)
    log_teacher = cached - jax.nn.logsumexp(cached, axis=1, keepdims=True)
    prob_teacher = jnp.exp(log_teacher)
    kl_loss = jnp.sum(prob_teacher * (log_teacher - log_student), axis=1)
    dscore = (50.0 * (jnp.exp(log_student) - prob_teacher)).astype(jnp.bfloat16)
    spread = jnp.sum(
        jnp.where(chosen, dscore.reshape(picks, offset_count, 1).astype(jnp.float32), 0.0), axis=1
    ).astype(jnp.bfloat16)
    dense = jnp.dot(place, spread, preferred_element_type=jnp.float32).astype(jnp.bfloat16)
    got_dense = lax.all_to_all(
        dense.reshape(n_corpus, slots_each, ROWS), "corpus", 0, 0, tiled=True
    ).reshape(slot_total, ROWS)
    expanded = jnp.concatenate(
        [jnp.where(slot_block == j, got_dense, jnp.bfloat16(0)) for j in range(blocks_here)], axis=1
    )
    block_part = jnp.dot(expanded, passages, preferred_element_type=jnp.float32).astype(
        jnp.bfloat16
    )
    arrived = lax.all_to_all(
        block_part.reshape(n_corpus, slots_each, cols), "corpus", 0, 0, tiled=True
    ).reshape(slot_total, cols)
    query_grad = lax.dot_general(
        owner, arrived, (((0,), (0,)), ((), ())), preferred_element_type=jnp.float32
    ).astype(jnp.bfloat16)
    grad_mine = lax.all_gather(query_grad, "corpus", axis=0, tiled=True)
    grad_theirs = lax.ppermute(grad_mine, "fsdp", SWAP)
    across = (((0,), (0,)), ((), ()))
    head_grad = lax.dot_general(
        all_mine, grad_mine, across, preferred_element_type=jnp.float32
    ) + lax.dot_general(all_theirs, grad_theirs, across, preferred_element_type=jnp.float32)
    return (kl_loss, head_grad)


def solution(mesh):
    placed = (
        P(("corpus", "fsdp"), None),
        P("fsdp", "tensor"),
        P("corpus", "tensor"),
        P(("corpus", "fsdp"), None, None),
        P(("corpus", "fsdp"), None),
        P(("corpus", "fsdp"), None, None),
        P(),
    )
    return jax.shard_map(
        on_device,
        mesh=mesh,
        in_specs=placed,
        out_specs=(P(("corpus", "fsdp")), P("fsdp", "tensor")),
        check_vma=False,
    )
```

profile of v0, /device:TPU:1, one launch (start us, length us, event | category | flops | bytes accessed | tf_op | source)
XLA Modules:
  0.0 353.7 jit_solution(15698942265412292982)
XLA Ops:
  7.2 0.0 copy-start
  7.2 2.2 broadcast_select_fusion
  9.4 1.4 collective-permute-start
  10.8 0.0 copy-done.6
  10.8 0.1 copy.18
  10.9 0.1 eq.213
  11.0 1.5 collective-permute-done
  12.5 3.9 %fusion.26 = f32[128,1024]{1,0:T(8,128)} fusion(bf16[128,2048]{1,0:T(8,128)(2,1)S(1)} %collective-permute-done, bf16[2048,1024]{1,0:T(8,128)(2,1)} %param.8), kind=kOutput, calls=%fused_computation.91 | convolution fusion | flops 536870912 | bytes 5242880 | tf_op jit(solution)/shard_map/dot_general | solution.py:28
  16.5 0.0 copy-done.3
  16.5 0.4 collective-permute-start.1
  16.8 0.2 select_reduce_fusion.2
  17.1 0.3 fusion.2
  17.4 0.1 add.152
  17.5 0.2 slice_reduce_fusion.3
  17.8 1.0 collective-permute-done.1
  18.7 4.6 %convolution_convert_fusion = bf16[768,1024]{1,0:T(8,128)(2,1)} fusion(f32[128,1024]{1,0:T(8,128)} %collective-permute-done.1, s32[128]{0:T(128)S(1)} %get-tuple-element.3, s32[128]{0:T(128)S(1)} %get-tuple-element.4, s32[128]{0:T(128)S(1)} %get-tuple-element.5, s32[128]{0:T(128)S(1)} %get-tuple-element.2, bf16[128,2048]{1,0:T(8,128)(2,1)S(1)} %get-tuple-element.9, ...), kind=kOutput, calls=%fused_computation.5 | convolution fusion | flops 739934208 | bytes 6817792 | tf_op jit(solution)/shard_map/dot_general | solution.py:53
  23.3 7.9 %all-to-all-start = ((bf16[16,48,1024]{2,1,0:T(8,128)(2,1)}), bf16[16,48,1024]{2,1,0:T(8,128)(2,1)}, u32[]{:S(2)}, u32[]{:S(2)}) async-start(bf16[16,48,1024]{2,1,0:T(8,128)(2,1)} %bitcast.46), calls=%async_computation | async-start | bytes 3145728 | tf_op jit(solution)/shard_map/all_to_all | solution.py:54
  31.4 23.9 %all-to-all-done = bf16[16,48,1024]{2,1,0:T(8,128)(2,1)} async-done(((bf16[16,48,1024]{2,1,0:T(8,128)(2,1)}), bf16[16,48,1024]{2,1,0:T(8,128)(2,1)}, u32[]{:S(2)}, u32[]{:S(2)}) %all-to-all-start) | async-done | bytes 1572896 | tf_op jit(solution)/shard_map/all_to_all | solution.py:54
  55.3 3.2 fusion.27
  58.5 0.0 copy-start.5
  58.6 0.0 copy-start.4
  58.6 2.1 fusion.9
  60.7 4.1 %all-to-all-start.1 = ((f32[16,48,128]{2,1,0:T(8,128)}), f32[16,48,128]{2,1,0:T(8,128)S(1)}, u32[]{:S(2)}, u32[]{:S(2)}) async-start(f32[16,48,128]{2,1,0:T(8,128)} %bitcast.4), calls=%async_computation.1 | async-start | bytes 786432 | tf_op jit(solution)/shard_map/all_to_all | solution.py:63
  64.8 0.1 copy.17
  65.0 8.7 %all-to-all-done.1 = f32[16,48,128]{2,1,0:T(8,128)S(1)} async-done(((f32[16,48,128]{2,1,0:T(8,128)}), f32[16,48,128]{2,1,0:T(8,128)S(1)}, u32[]{:S(2)}, u32[]{:S(2)}) %all-to-all-start.1) | async-done | bytes 393248 | tf_op jit(solution)/shard_map/all_to_all | solution.py:63
  73.8 1.0 gather_fusion
  74.8 5.1 %select_reduce_fusion.1 = f32[512,32]{1,0:T(8,128)S(1)} fusion(f32[512,128]{1,0:T(8,128)S(1)} %gather_fusion, s32[512,32]{1,0:T(8,128)S(1)} %bitcast.47), kind=kLoop, calls=%fused_computation.2 | loop fusion | flops 6275072 | bytes 393216 | tf_op jit(solution)/shard_map/reduce_sum | solution.py:70
  79.9 0.1 reshape.196
  80.0 0.1 copy.20
  80.1 1.3 collective-permute-start.2
  81.5 1.9 collective-permute-done.2
  83.3 2.8 collective-permute-start.3
  86.2 2.6 collective-permute-done.3
  88.8 0.6 fusion.18
  89.4 0.1 copy.21
  89.5 0.1 reshape.201
  89.6 5.6 %select_reduce_fusion = bf16[512,128]{1,0:T(8,128)(2,1)S(1)} fusion(f32[512,32]{1,0:T(8,128)S(1)} %reshape.201, s32[512,32]{1,0:T(8,128)S(1)} %bitcast.48), kind=kLoop, calls=%fused_computation.1 | loop fusion | flops 6225920 | bytes 262144 | tf_op jit(solution)/shard_map/reduce_sum | solution.py:81
  95.2 1.1 fusion.1
  96.3 3.5 all-to-all-start.2
  99.8 0.0 all-gather.6.cloned.1.call-start
  99.9 7.1 %all-to-all-done.2 = bf16[16,48,128]{2,1,0:T(8,128)(2,1)S(1)} async-done(((bf16[16,48,128]{2,1,0:T(8,128)(2,1)}), bf16[16,48,128]{2,1,0:T(8,128)(2,1)S(1)}, u32[]{:S(2)}, u32[]{:S(2)}) %all-to-all-start.2) | async-done | bytes 196640 | tf_op jit(solution)/shard_map/all_to_all | solution.py:85
  107.0 1.2 bitcast_select_fusion
  108.2 0.1 constant_dynamic-update-slice_fusion.6
  108.3 0.1 constant_dynamic-update-slice_fusion.5
  108.4 0.1 constant_dynamic-update-slice_fusion.4
  108.4 0.1 constant_dynamic-update-slice_fusion.3
  108.5 0.1 constant_dynamic-update-slice_fusion.2
  108.6 0.1 constant_dynamic-update-slice_fusion.1
  108.6 0.1 constant_dynamic-update-slice_fusion
  108.7 1.8 convolution_convert_fusion.1
  110.5 21.1 %all_to_all.20 = bf16[16,48,1024]{2,1,0:T(8,128)(2,1)S(1)} all-to-all(bf16[16,48,1024]{2,1,0:T(8,128)(2,1)S(1)} %bitcast.50), channel_id=1, replica_groups=mesh['corpus'=16,'fsdp'=2,'tensor'=4] {'corpus'}, dimensions={0} | all-to-all | bytes 3145728 | tf_op jit(solution)/shard_map/all_to_all | solution.py:94
  131.6 1.2 convolution_convert_fusion.2
  132.8 0.0 all-gather.6.cloned.1.call-update
  132.8 0.0 all-gather.4.cloned.1.call-start
  132.9 0.7 all-gather.4.cloned.1.call-update
  133.6 0.0 all-gather.8.cloned.1.call-start
  133.6 0.7 all-gather.8.cloned.1.call-update
  134.3 51.5 %all-gather.6.cloned.1.call-done = bf16[2048,1024]{1,0:T(8,128)(2,1)} async-done(((bf16[128,1024]{1,0:T(8,128)(2,1)}), bf16[2048,1024]{1,0:T(8,128)(2,1)}) %all-gather.6.cloned.1.call-update) | async-done | bytes 4194320 | tf_op jit(solution)/shard_map/all_gather | solution.py:100
  185.8 0.8 collective-permute-start.4
  186.6 71.8 %all-gather.4.cloned.1.call-done = bf16[2048,2048]{1,0:T(8,128)(2,1)} async-done(((bf16[128,2048]{1,0:T(8,128)(2,1)}), bf16[2048,2048]{1,0:T(8,128)(2,1)}) %all-gather.4.cloned.1.call-update) | async-done | bytes 8388624 | tf_op jit(solution)/shard_map/all_gather | solution.py:32
  258.5 14.6 %fusion.28 = f32[2048,1024]{1,0:T(8,128)} fusion(bf16[2048,2048]{1,0:T(8,128)(2,1)} %all-gather.4.cloned.1.call-done, bf16[2048,1024]{1,0:T(8,128)(2,1)} %all-gather.6.cloned.1.call-done), kind=kOutput, calls=%fused_computation.93 | convolution fusion | flops 8589934592 | bytes 20971520 | tf_op jit(solution)/shard_map/dot_general | solution.py:103
  273.1 58.1 %all-gather.8.cloned.1.call-done = bf16[2048,2048]{1,0:T(8,128)(2,1)} async-done(((bf16[128,2048]{1,0:T(8,128)(2,1)}), bf16[2048,2048]{1,0:T(8,128)(2,1)}) %all-gather.8.cloned.1.call-update) | async-done | bytes 8388624 | tf_op jit(solution)/shard_map/all_gather | solution.py:33
  331.2 0.0 collective-permute-done.4
  331.2 16.0 %convolution_add_fusion = f32[2048,1024]{1,0:T(8,128)} fusion(f32[2048,1024]{1,0:T(8,128)} %fusion.28, bf16[2048,2048]{1,0:T(8,128)(2,1)} %all-gather.8.cloned.1.call-done, bf16[2048,1024]{1,0:T(8,128)(2,1)} %collective-permute-done.4), kind=kOutput, calls=%fused_computation.4 | convolution fusion | flops 8592031744 | bytes 29360128 | tf_op jit(solution)/shard_map/dot_general | solution.py:105
  (29 shorter events, 0.4 us)
Async XLA Ops:
  7.2 48.1 %copy-start = (bf16[1024,1024]{1,0:T(8,128)(2,1)S(1)}, bf16[1024,1024]{1,0:T(8,128)(2,1)}, u32[]{:S(2)}) copy-start(bf16[1024,1024]{1,0:T(8,128)(2,1)} %param.9) | copy-start | bytes 6291460
  7.2 3.6 %copy-start.6 = (s32[128,4]{0,1:T(4,128)S(1)}, s32[128,4]{0,1:T(4,128)}, u32[]{:S(2)}) copy-start(s32[128,4]{0,1:T(4,128)} %param.11) | copy-start | bytes 6148
  9.4 9.3 %copy-start.2 = (bf16[128,2048]{1,0:T(8,128)(2,1)}, bf16[128,2048]{1,0:T(8,128)(2,1)S(1)}, u32[]{:S(2)}) copy-start(bf16[128,2048]{1,0:T(8,128)(2,1)S(1)} %get-tuple-element.9) | copy-start | bytes 1572868
  9.4 3.1 collective-permute-start
  12.5 3.9 %copy-start.3 = (bf16[128,2048]{1,0:T(8,128)(2,1)}, bf16[128,2048]{1,0:T(8,128)(2,1)S(1)}, u32[]{:S(2)}) copy-start(bf16[128,2048]{1,0:T(8,128)(2,1)S(1)} %collective-permute-done) | copy-start | bytes 1572868
  12.5 4.3 %copy-start.7 = (s32[128]{0:T(128)S(1)}, s32[128]{0:T(128)}, u32[]{:S(2)}) copy-start(s32[128]{0:T(128)} %param.13) | copy-start | bytes 1540
  16.5 2.3 collective-permute-start.1
  23.3 32.0 %all-to-all-start = ((bf16[16,48,1024]{2,1,0:T(8,128)(2,1)}), bf16[16,48,1024]{2,1,0:T(8,128)(2,1)}, u32[]{:S(2)}, u32[]{:S(2)}) async-start(bf16[16,48,1024]{2,1,0:T(8,128)(2,1)} %bitcast.46), calls=%async_computation | async-start | bytes 3145728 | tf_op jit(solution)/shard_map/all_to_all | solution.py:54
  58.5 6.2 %copy-start.5 = (s32[128,4,32]{0,2,1:T(8,128)S(1)}, s32[128,4,32]{0,2,1:T(8,128)}, u32[]{:S(2)}) copy-start(s32[128,4,32]{0,2,1:T(8,128)} %param.12) | copy-start | bytes 196612
  58.6 6.4 %copy-start.4 = (f32[128,4,32]{0,2,1:T(8,128)S(1)}, f32[128,4,32]{0,2,1:T(8,128)}, u32[]{:S(2)}) copy-start(f32[128,4,32]{0,2,1:T(8,128)} %param.10) | copy-start | bytes 196612
  60.7 13.1 %all-to-all-start.1 = ((f32[16,48,128]{2,1,0:T(8,128)}), f32[16,48,128]{2,1,0:T(8,128)S(1)}, u32[]{:S(2)}, u32[]{:S(2)}) async-start(f32[16,48,128]{2,1,0:T(8,128)} %bitcast.4), calls=%async_computation.1 | async-start | bytes 786432 | tf_op jit(solution)/shard_map/all_to_all | solution.py:63
  80.1 3.2 collective-permute-start.2
  83.3 5.4 %collective-permute-start.3 = (f32[128,128]{0,1:T(8,128)S(1)}, f32[128,128]{0,1:T(8,128)S(1)}, u32[]{:S(2)}, u32[]{:S(2)}) collective-permute-start(f32[128,128]{0,1:T(8,128)S(1)} %add.157), channel_id=1, source_target_pairs={{0,2},{2,0},{1,3},{3,1},{4,6},{6,4},{5,7},{7,5},{8,10},{10,8},{9,1... | collective-permute-start | bytes 196616 | tf_op jit(solution)/shard_map/ppermute | solution.py:73
  96.3 10.7 %all-to-all-start.2 = ((bf16[16,48,128]{2,1,0:T(8,128)(2,1)}), bf16[16,48,128]{2,1,0:T(8,128)(2,1)S(1)}, u32[]{:S(2)}, u32[]{:S(2)}) async-start(bf16[16,48,128]{2,1,0:T(8,128)(2,1)} %bitcast.8), calls=%async_computation.2 | async-start | bytes 393216 | tf_op jit(solution)/shard_map/all_to_all | solution.py:85
  99.8 85.9 %all-gather.6.cloned.1.call-start = ((), (), s32[]{:S(2)}) async-start(), calls=%async_computation.5 | async-start | bytes 4456448 | tf_op jit(solution)/shard_map/all_gather | solution.py:100
  132.8 125.6 %all-gather.4.cloned.1.call-start = ((), (), s32[]{:S(2)}) async-start(), calls=%async_computation.4 | async-start | bytes 8912896 | tf_op jit(solution)/shard_map/all_gather | solution.py:32
  133.6 197.6 %all-gather.8.cloned.1.call-start = ((), (), s32[]{:S(2)}) async-start(), calls=%async_computation.6 | async-start | bytes 8912896 | tf_op jit(solution)/shard_map/all_gather | solution.py:33
  185.8 145.4 %collective-permute-start.4 = (bf16[2048,1024]{1,0:T(8,128)(2,1)}, bf16[2048,1024]{1,0:T(8,128)(2,1)}, u32[]{:S(2)}, u32[]{:S(2)}) collective-permute-start(bf16[2048,1024]{1,0:T(8,128)(2,1)} %all-gather.6.cloned.1.call-done), channel_id=1, source_target_pairs={{0,4},{4,0},{1,5},{5,1},{2,6},{6,2},{3,7},{7,3},{8,12},{12,8},{9,1... | collective-permute-start | bytes 12582920 | tf_op jit(solution)/shard_map/ppermute | solution.py:101
  331.2 16.0 %copy-start.1 = (bf16[1024,1024]{1,0:T(8,128)(2,1)S(1)}, bf16[1024,1024]{1,0:T(8,128)(2,1)}, u32[]{:S(2)}) copy-start(bf16[1024,1024]{1,0:T(8,128)(2,1)} %param.9) | copy-start | bytes 6291460
Sparse Core Ops, SparseCore 0:
  132.9 52.7 all-gather.5
  187.9 70.5 all-gather.3
  260.6 70.5 all-gather.7
where the time goes:
time: 354 us
  waiting for transfers between devices  229 us (65%)
  matrix products  46.7 us (13%)
  starting transfers between devices  22.4 us (6%)
  blocking collectives  21.1 us (6%)
  other arithmetic  17.3 us (5%)
  between operations  14 us (4%)
    all_gather x1, waiting for transfers between devices, on_device(): all_mine = lax.all_gather(mine, 'corpus', axis=0, tiled=True)  71.8 us
    all_gather x1, waiting for transfers between devices, on_device(): all_theirs = lax.all_gather(theirs, 'corpus', axis=0, tiled=True)  58.1 us
    all_gather x1, waiting for transfers between devices, on_device(): grad_mine = lax.all_gather(query_grad, 'corpus', axis=0, tiled=True)  51.5 us
    all_to_all x1, waiting for transfers between devices, on_device(): lax.all_to_all(send_queries.reshape(n_corpus, slots_each, cols), 'corpus'...  23.9 us
    all_to_all x1, blocking collectives, on_device(): lax.all_to_all(block_part.reshape(n_corpus, slots_each, cols), 'corpus',...  21.1 us
    dot_general x1, matrix products, on_device(): lax.dot_general(all_theirs, grad_theirs, across, preferred_element_type=j...  16 us
    dot_general x1, matrix products, on_device(): lax.dot_general(all_mine, grad_mine, across, preferred_element_type=jnp.f...  14.6 us
    all_to_all x1, waiting for transfers between devices, on_device(): lax.all_to_all(scores.reshape(n_corpus, slots_each, ROWS), 'corpus', 0, 0...  8.74 us
  transfers between devices with their start and end apart: 11, of which 10 were waited for; matrix products, arithmetic and copies ran while one was open for 5% of the time, Pallas kernels for 0%

commit v1 on v0

--- a/solution.py
+++ b/solution.py
@@ -6,6 +6,28 @@
 ROWS = 128
 MOSTB = 6
 SWAP = [(0, 1), (1, 0)]
+
+
+def laid_out(blocks, dim):
+    dims = list(blocks.shape[1:])
+    dims[dim] *= blocks.shape[0]
+    return jnp.moveaxis(blocks, 0, dim).reshape(dims)
+
+
+def gather_around(x, axis, dim):
+    size = lax.axis_size(axis)
+    pairs = [(i, (i + 1) % size) for i in range(size)]
+    back = [(b, a) for a, b in pairs]
+    lower, upper = ([], [])
+    for step in range(size - 1):
+        if step % 2 == 0:
+            lower.append(lax.ppermute(lower[-1] if lower else x, axis, pairs))
+        else:
+            upper.append(lax.ppermute(upper[-1] if upper else x, axis, back))
+    tiles = jnp.stack([*lower[::-1], x, *upper])
+    shift = lax.axis_index(axis) - len(lower)
+    tiles = tiles[(jnp.arange(size) - shift) % size]
+    return laid_out(tiles, dim)
 
 
 def on_device(queries_in, head_weight, passages, teacher, cand_block, cand_offset, block_slot):
@@ -97,7 +119,7 @@
     query_grad = lax.dot_general(
         owner, arrived, (((0,), (0,)), ((), ())), preferred_element_type=jnp.float32
     ).astype(jnp.bfloat16)
-    grad_mine = lax.all_gather(query_grad, "corpus", axis=0, tiled=True)
+    grad_mine = gather_around(query_grad, "corpus", 0)
     grad_theirs = lax.ppermute(grad_mine, "fsdp", SWAP)
     across = (((0,), (0,)), ((), ()))
     head_grad = lax.dot_general(

time: 354 us -> 329 us (0.929)
  waiting for transfers between devices: 229 us -> 122 us
  starting transfers between devices: 22.4 us -> 79.3 us
  local copies, waits for them, and re-layouts: 2.67 us -> 22.5 us
  blocking collectives: 21.1 us -> 27.3 us
    all_gather x1, waiting for transfers between devices: 71.8 us -> 0.01 us  [on_device(): all_mine = lax.all_gather(mine, 'corpus', axis=0, tiled=True)]
    ppermute x0 -> x15, waiting for transfers between devices: none -> 60.1 us  [the longest x8 47.2 us: gather_around(): lower.append(lax.ppermute(lower[-1] if lower else x, axis, pairs))]
    all_gather x1, waiting for transfers between devices: 58.1 us -> 0.01 us  [on_device(): all_theirs = lax.all_gather(theirs, 'corpus', axis=0, tiled=True)]
    all_gather x1 -> x0, waiting for transfers between devices: 51.5 us -> none  [on_device(): grad_mine = lax.all_gather(query_grad, 'corpus', axis=0, tiled=True)]
    ppermute x0 -> x15, starting transfers between devices: none -> 35.9 us  [the longest x7 35.5 us: gather_around(): upper.append(lax.ppermute(upper[-1] if upper else x, axis, back))]
    ppermute x1, starting transfers between devices: 0.84 us -> 20.3 us  [on_device(): grad_theirs = lax.ppermute(grad_mine, 'fsdp', SWAP)]
    unnamed x25 -> x38, local copies, waits for them, and re-layouts: 0.73 us -> 14.9 us
    ppermute x1, waiting for transfers between devices: 0.01 us -> 7.13 us  [on_device(): grad_theirs = lax.ppermute(grad_mine, 'fsdp', SWAP)]
  transfers between devices with their start and end apart: 11 -> 25, of which waited for: 10 -> 19; matrix products, arithmetic and copies ran while one was open for 5% -> 20% of each run, Pallas kernels for 0% -> 0%
where the time goes in v1:
time: 329 us; the launch traced here: 328 us
  waiting for transfers between devices  122 us (37%)
  starting transfers between devices  79.3 us (24%)
  matrix products  45.8 us (14%)
  blocking collectives  27.3 us (8%)
  local copies, waits for them, and re-layouts  22.5 us (7%)
  other arithmetic  16.5 us (5%)
  between operations  14.4 us (4%)
    ppermute x8, waiting for transfers between devices, gather_around(): lower.append(lax.ppermute(lower[-1] if lower else x, axis, pairs))  47.2 us
    ppermute x7, starting transfers between devices, gather_around(): upper.append(lax.ppermute(upper[-1] if upper else x, axis, back))  35.5 us
    all_to_all x1, blocking collectives, on_device(): lax.all_to_all(block_part.reshape(n_corpus, slots_each, cols), 'corpus',...  27.3 us
    all_to_all x1, waiting for transfers between devices, on_device(): lax.all_to_all(send_queries.reshape(n_corpus, slots_each, cols), 'corpus'...  27.2 us
    ppermute x1, starting transfers between devices, on_device(): grad_theirs = lax.ppermute(grad_mine, 'fsdp', SWAP)  20.3 us
    dot_general x1, matrix products, on_device(): lax.dot_general(all_mine, grad_mine, across, preferred_element_type=jnp.f...  16 us
    unnamed x38, local copies, waits for them, and re-layouts  14.9 us
    dot_general x1, matrix products, on_device(): lax.dot_general(all_theirs, grad_theirs, across, preferred_element_type=j...  14.6 us
  transfers between devices with their start and end apart: 25, of which 19 were waited for; matrix products, arithmetic and copies ran while one was open for 20% of the time, Pallas kernels for 0%

profile of v1, /device:TPU:1, one launch (start us, length us, event | category | flops | bytes accessed | tf_op | source)
XLA Modules:
  0.0 328.2 jit_solution(8228447870690326612)
XLA Ops:
  7.2 1.4 broadcast_select_fusion
  8.7 1.5 collective-permute-start
  10.1 1.5 collective-permute-done
  11.7 0.8 copy-done.3
  12.5 0.8 copy.18
  13.4 3.9 %fusion.28 = f32[128,1024]{1,0:T(8,128)} fusion(bf16[128,2048]{1,0:T(8,128)(2,1)} %copy-done.3, bf16[2048,1024]{1,0:T(8,128)(2,1)} %param.8), kind=kOutput, calls=%fused_computation.115 | convolution fusion | flops 536870912 | bytes 5242880 | tf_op jit(solution)/shard_map/dot_general | solution.py:50
  18.6 0.8 collective-permute-done.1
  19.4 4.5 %convolution_convert_fusion = bf16[768,1024]{1,0:T(8,128)(2,1)} fusion(f32[128,1024]{1,0:T(8,128)S(1)} %collective-permute-done.1, s32[128]{0:T(128)S(1)} %get-tuple-element.3, s32[128]{0:T(128)S(1)} %get-tuple-element.4, s32[128]{0:T(128)S(1)} %get-tuple-element.5, s32[128]{0:T(128)S(1)} %get-tuple-element.2, bf16[128,2048]{1,0:T(8,128)(2,1)S(1)} %get-tuple-element.9, ...), kind=kOutput, calls=%fused_computation.6 | convolution fusion | flops 739934208 | bytes 6817792 | tf_op jit(solution)/shard_map/dot_general | solution.py:75
  23.9 7.9 %all-to-all-start = ((bf16[16,48,1024]{2,1,0:T(8,128)(2,1)}), bf16[16,48,1024]{2,1,0:T(8,128)(2,1)}, u32[]{:S(2)}, u32[]{:S(2)}) async-start(bf16[16,48,1024]{2,1,0:T(8,128)(2,1)} %bitcast.81), calls=%async_computation | async-start | bytes 3145728 | tf_op jit(solution)/shard_map/all_to_all | solution.py:76
  31.9 27.2 %all-to-all-done = bf16[16,48,1024]{2,1,0:T(8,128)(2,1)} async-done(((bf16[16,48,1024]{2,1,0:T(8,128)(2,1)}), bf16[16,48,1024]{2,1,0:T(8,128)(2,1)}, u32[]{:S(2)}, u32[]{:S(2)}) %all-to-all-start) | async-done | bytes 1572896 | tf_op jit(solution)/shard_map/all_to_all | solution.py:76
  59.1 3.2 fusion.29
  62.3 2.1 fusion.9
  64.5 5.6 %all-to-all-start.1 = ((f32[16,48,128]{2,1,0:T(8,128)}), f32[16,48,128]{2,1,0:T(8,128)S(1)}, u32[]{:S(2)}, u32[]{:S(2)}) async-start(f32[16,48,128]{2,1,0:T(8,128)} %bitcast.4), calls=%async_computation.1 | async-start | bytes 786432 | tf_op jit(solution)/shard_map/all_to_all | solution.py:85
  70.3 14.0 %all-to-all-done.1 = f32[16,48,128]{2,1,0:T(8,128)S(1)} async-done(((f32[16,48,128]{2,1,0:T(8,128)}), f32[16,48,128]{2,1,0:T(8,128)S(1)}, u32[]{:S(2)}, u32[]{:S(2)}) %all-to-all-start.1) | async-done | bytes 393248 | tf_op jit(solution)/shard_map/all_to_all | solution.py:85
  84.2 1.0 gather_fusion
  85.3 5.1 %select_reduce_fusion.1 = f32[512,32]{1,0:T(8,128)S(1)} fusion(f32[512,128]{1,0:T(8,128)S(1)} %gather_fusion, s32[512,32]{1,0:T(8,128)S(1)} %bitcast.84), kind=kLoop, calls=%fused_computation.3 | loop fusion | flops 6275072 | bytes 393216 | tf_op jit(solution)/shard_map/reduce_sum | solution.py:92
  90.6 1.4 collective-permute-start.2
  92.0 2.2 collective-permute-done.2
  94.2 2.8 collective-permute-start.3
  97.0 2.3 collective-permute-done.3
  100.2 5.6 %select_reduce_fusion = bf16[512,128]{1,0:T(8,128)(2,1)S(1)} fusion(f32[512,32]{1,0:T(8,128)S(1)} %reshape.254, s32[512,32]{1,0:T(8,128)S(1)} %bitcast.85), kind=kLoop, calls=%fused_computation.2 | loop fusion | flops 6225920 | bytes 262144 | tf_op jit(solution)/shard_map/reduce_sum | solution.py:103
  105.9 1.1 fusion.1
  106.9 3.5 %all-to-all-start.2 = ((bf16[16,48,128]{2,1,0:T(8,128)(2,1)}), bf16[16,48,128]{2,1,0:T(8,128)(2,1)S(1)}, u32[]{:S(2)}, u32[]{:S(2)}) async-start(bf16[16,48,128]{2,1,0:T(8,128)(2,1)} %bitcast.8), calls=%async_computation.2 | async-start | bytes 393216 | tf_op jit(solution)/shard_map/all_to_all | solution.py:107
  111.2 6.4 %all-to-all-done.2 = bf16[16,48,128]{2,1,0:T(8,128)(2,1)S(1)} async-done(((bf16[16,48,128]{2,1,0:T(8,128)(2,1)}), bf16[16,48,128]{2,1,0:T(8,128)(2,1)S(1)}, u32[]{:S(2)}, u32[]{:S(2)}) %all-to-all-start.2) | async-done | bytes 196640 | tf_op jit(solution)/shard_map/all_to_all | solution.py:107
  117.6 1.2 bitcast_select_fusion
  119.3 1.8 convolution_convert_fusion.1
  121.2 27.3 %all_to_all.20 = bf16[16,48,1024]{2,1,0:T(8,128)(2,1)S(1)} all-to-all(bf16[16,48,1024]{2,1,0:T(8,128)(2,1)S(1)} %bitcast.87), channel_id=1, replica_groups=mesh['corpus'=16,'fsdp'=2,'tensor'=4] {'corpus'}, dimensions={0} | all-to-all | bytes 3145728 | tf_op jit(solution)/shard_map/all_to_all | solution.py:116
  149.3 8.5 %collective-permute-done.4 = bf16[128,1024]{1,0:T(8,128)(2,1)S(1)} collective-permute-done((bf16[128,1024]{1,0:T(8,128)(2,1)S(1)}, bf16[128,1024]{1,0:T(8,128)(2,1)S(1)}, u32[]{:S(2)}, u32[]{:S(2)}) %collective-permute-start.4) | collective-permute-done | bytes 262176 | tf_op jit(solution)/shard_map/ppermute | solution.py:24
  157.7 4.8 %collective-permute-start.12 = (bf16[128,1024]{1,0:T(8,128)(2,1)S(1)}, bf16[128,1024]{1,0:T(8,128)(2,1)S(1)}, u32[]{:S(2)}, u32[]{:S(2)}) collective-permute-start(bf16[128,1024]{1,0:T(8,128)(2,1)S(1)} %convolution_convert_fusion.2), channel_id=1, source_target_pairs={{8,0},{16,8},{24,16},{32,24},{40,32},{48,40},{56,48},{64,56},{72,6... | collective-permute-start | bytes 786440 | tf_op jit(solution)/shard_map/ppermute | solution.py:26
  162.5 5.7 %collective-permute-done.5 = bf16[128,1024]{1,0:T(8,128)(2,1)S(1)} collective-permute-done((bf16[128,1024]{1,0:T(8,128)(2,1)S(1)}, bf16[128,1024]{1,0:T(8,128)(2,1)S(1)}, u32[]{:S(2)}, u32[]{:S(2)}) %collective-permute-start.5) | collective-permute-done | bytes 262176 | tf_op jit(solution)/shard_map/ppermute | solution.py:24
  168.2 3.3 %collective-permute-done.12 = bf16[128,1024]{1,0:T(8,128)(2,1)S(1)} collective-permute-done((bf16[128,1024]{1,0:T(8,128)(2,1)S(1)}, bf16[128,1024]{1,0:T(8,128)(2,1)S(1)}, u32[]{:S(2)}, u32[]{:S(2)}) %collective-permute-start.12) | collective-permute-done | bytes 262176 | tf_op jit(solution)/shard_map/ppermute | solution.py:26
  171.6 5.2 %collective-permute-start.13 = (bf16[128,1024]{1,0:T(8,128)(2,1)S(1)}, bf16[128,1024]{1,0:T(8,128)(2,1)S(1)}, u32[]{:S(2)}, u32[]{:S(2)}) collective-permute-start(bf16[128,1024]{1,0:T(8,128)(2,1)S(1)} %collective-permute-done.12), channel_id=1, source_target_pairs={{8,0},{16,8},{24,16},{32,24},{40,32},{48,40},{56,48},{64,56},{72,6... | collective-permute-start | bytes 786440 | tf_op jit(solution)/shard_map/ppermute | solution.py:26
  176.8 6.4 %collective-permute-done.6 = bf16[128,1024]{1,0:T(8,128)(2,1)S(1)} collective-permute-done((bf16[128,1024]{1,0:T(8,128)(2,1)S(1)}, bf16[128,1024]{1,0:T(8,128)(2,1)S(1)}, u32[]{:S(2)}, u32[]{:S(2)}) %collective-permute-start.6) | collective-permute-done | bytes 262176 | tf_op jit(solution)/shard_map/ppermute | solution.py:24
  183.2 4.2 %collective-permute-done.13 = bf16[128,1024]{1,0:T(8,128)(2,1)S(1)} collective-permute-done((bf16[128,1024]{1,0:T(8,128)(2,1)S(1)}, bf16[128,1024]{1,0:T(8,128)(2,1)S(1)}, u32[]{:S(2)}, u32[]{:S(2)}) %collective-permute-start.13) | collective-permute-done | bytes 262176 | tf_op jit(solution)/shard_map/ppermute | solution.py:26
  187.4 5.5 %collective-permute-start.14 = (bf16[128,1024]{1,0:T(8,128)(2,1)S(1)}, bf16[128,1024]{1,0:T(8,128)(2,1)S(1)}, u32[]{:S(2)}, u32[]{:S(2)}) collective-permute-start(bf16[128,1024]{1,0:T(8,128)(2,1)S(1)} %collective-permute-done.13), channel_id=1, source_target_pairs={{8,0},{16,8},{24,16},{32,24},{40,32},{48,40},{56,48},{64,56},{72,6... | collective-permute-start | bytes 786440 | tf_op jit(solution)/shard_map/ppermute | solution.py:26
  193.0 5.2 %collective-permute-done.7 = bf16[128,1024]{1,0:T(8,128)(2,1)S(1)} collective-permute-done((bf16[128,1024]{1,0:T(8,128)(2,1)S(1)}, bf16[128,1024]{1,0:T(8,128)(2,1)S(1)}, u32[]{:S(2)}, u32[]{:S(2)}) %collective-permute-start.7) | collective-permute-done | bytes 262176 | tf_op jit(solution)/shard_map/ppermute | solution.py:24
  198.2 5.3 %collective-permute-done.14 = bf16[128,1024]{1,0:T(8,128)(2,1)S(1)} collective-permute-done((bf16[128,1024]{1,0:T(8,128)(2,1)S(1)}, bf16[128,1024]{1,0:T(8,128)(2,1)S(1)}, u32[]{:S(2)}, u32[]{:S(2)}) %collective-permute-start.14) | collective-permute-done | bytes 262176 | tf_op jit(solution)/shard_map/ppermute | solution.py:26
  203.4 5.5 %collective-permute-start.15 = (bf16[128,1024]{1,0:T(8,128)(2,1)S(1)}, bf16[128,1024]{1,0:T(8,128)(2,1)S(1)}, u32[]{:S(2)}, u32[]{:S(2)}) collective-permute-start(bf16[128,1024]{1,0:T(8,128)(2,1)S(1)} %collective-permute-done.14), channel_id=1, source_target_pairs={{8,0},{16,8},{24,16},{32,24},{40,32},{48,40},{56,48},{64,56},{72,6... | collective-permute-start | bytes 786440 | tf_op jit(solution)/shard_map/ppermute | solution.py:26
  209.0 4.1 %collective-permute-done.8 = bf16[128,1024]{1,0:T(8,128)(2,1)S(1)} collective-permute-done((bf16[128,1024]{1,0:T(8,128)(2,1)S(1)}, bf16[128,1024]{1,0:T(8,128)(2,1)S(1)}, u32[]{:S(2)}, u32[]{:S(2)}) %collective-permute-start.8) | collective-permute-done | bytes 262176 | tf_op jit(solution)/shard_map/ppermute | solution.py:24
  213.0 4.8 %collective-permute-start.16 = (bf16[128,1024]{1,0:T(8,128)(2,1)S(1)}, bf16[128,1024]{1,0:T(8,128)(2,1)S(1)}, u32[]{:S(2)}, u32[]{:S(2)}) collective-permute-start(bf16[128,1024]{1,0:T(8,128)(2,1)S(1)} %collective-permute-done.15), channel_id=1, source_target_pairs={{8,0},{16,8},{24,16},{32,24},{40,32},{48,40},{56,48},{64,56},{72,6... | collective-permute-start | bytes 786440 | tf_op jit(solution)/shard_map/ppermute | solution.py:26
  217.8 4.7 %collective-permute-done.9 = bf16[128,1024]{1,0:T(8,128)(2,1)S(1)} collective-permute-done((bf16[128,1024]{1,0:T(8,128)(2,1)S(1)}, bf16[128,1024]{1,0:T(8,128)(2,1)S(1)}, u32[]{:S(2)}, u32[]{:S(2)}) %collective-permute-start.9) | collective-permute-done | bytes 262176 | tf_op jit(solution)/shard_map/ppermute | solution.py:24
  222.5 4.8 %collective-permute-start.17 = (bf16[128,1024]{1,0:T(8,128)(2,1)S(1)}, bf16[128,1024]{1,0:T(8,128)(2,1)S(1)}, u32[]{:S(2)}, u32[]{:S(2)}) collective-permute-start(bf16[128,1024]{1,0:T(8,128)(2,1)S(1)} %collective-permute-done.16), channel_id=1, source_target_pairs={{8,0},{16,8},{24,16},{32,24},{40,32},{48,40},{56,48},{64,56},{72,6... | collective-permute-start | bytes 786440 | tf_op jit(solution)/shard_map/ppermute | solution.py:26
  227.2 5.9 %collective-permute-done.10 = bf16[128,1024]{1,0:T(8,128)(2,1)} collective-permute-done((bf16[128,1024]{1,0:T(8,128)(2,1)S(1)}, bf16[128,1024]{1,0:T(8,128)(2,1)}, u32[]{:S(2)}, u32[]{:S(2)}) %collective-permute-start.10) | collective-permute-done | bytes 262176 | tf_op jit(solution)/shard_map/ppermute | solution.py:24
  233.2 4.9 %collective-permute-start.18 = (bf16[128,1024]{1,0:T(8,128)(2,1)S(1)}, bf16[128,1024]{1,0:T(8,128)(2,1)S(1)}, u32[]{:S(2)}, u32[]{:S(2)}) collective-permute-start(bf16[128,1024]{1,0:T(8,128)(2,1)S(1)} %collective-permute-done.17), channel_id=1, source_target_pairs={{8,0},{16,8},{24,16},{32,24},{40,32},{48,40},{56,48},{64,56},{72,6... | collective-permute-start | bytes 786440 | tf_op jit(solution)/shard_map/ppermute | solution.py:26
  238.1 6.8 %collective-permute-done.11 = bf16[128,1024]{1,0:T(8,128)(2,1)} collective-permute-done((bf16[128,1024]{1,0:T(8,128)(2,1)}, bf16[128,1024]{1,0:T(8,128)(2,1)}, u32[]{:S(2)}, u32[]{:S(2)}) %collective-permute-start.11) | collective-permute-done | bytes 262176 | tf_op jit(solution)/shard_map/ppermute | solution.py:24
  244.9 1.7 bitcast_dynamic-update-slice_fusion.15
  246.6 1.7 bitcast_dynamic-update-slice_fusion.14
  248.3 0.7 bitcast_dynamic-update-slice_fusion.13
  249.0 0.7 bitcast_dynamic-update-slice_fusion.12
  249.7 0.7 bitcast_dynamic-update-slice_fusion.11
  250.4 0.7 bitcast_dynamic-update-slice_fusion.10
  251.2 0.7 bitcast_dynamic-update-slice_fusion.9
  251.9 0.7 bitcast_dynamic-update-slice_fusion.8
  252.6 0.7 bitcast_dynamic-update-slice_fusion.7
  253.3 0.7 bitcast_dynamic-update-slice_fusion.6
  254.0 0.7 bitcast_dynamic-update-slice_fusion.5
  254.8 0.7 bitcast_dynamic-update-slice_fusion.4
  255.5 0.7 bitcast_dynamic-update-slice_fusion.3
  257.6 0.7 bitcast_dynamic-update-slice_fusion
  258.4 4.9 %gather_fusion.1 = bf16[16,128,1024]{2,1,0:T(8,128)(2,1)} fusion(bf16[16,128,1024]{2,1,0:T(8,128)(2,1)} %bitcast_dynamic-update-slice_fusion, s32[1024]{0:T(1024)S(1)} %pad_clamp_fusion), kind=kCustom, calls=%fused_computation.1 | custom fusion | bytes 8388672 | tf_op jit(solution)/shard_map/gather | solution.py:29
  263.3 20.3 %collective-permute-start.19 = (bf16[2048,1024]{1,0:T(8,128)(2,1)}, bf16[2048,1024]{1,0:T(8,128)(2,1)}, u32[]{:S(2)}, u32[]{:S(2)}) collective-permute-start(bf16[2048,1024]{1,0:T(8,128)(2,1)} %bitcast.82), channel_id=1, source_target_pairs={{0,4},{4,0},{1,5},{5,1},{2,6},{6,2},{3,7},{7,3},{8,12},{12,8},{9,1... | collective-permute-start | bytes 12582920 | tf_op jit(solution)/shard_map/ppermute | solution.py:123
  283.6 7.1 %collective-permute-done.19 = bf16[2048,1024]{1,0:T(8,128)(2,1)} collective-permute-done((bf16[2048,1024]{1,0:T(8,128)(2,1)}, bf16[2048,1024]{1,0:T(8,128)(2,1)}, u32[]{:S(2)}, u32[]{:S(2)}) %collective-permute-start.19) | collective-permute-done | bytes 4194336 | tf_op jit(solution)/shard_map/ppermute | solution.py:123
  290.7 14.6 %fusion.30 = f32[2048,1024]{1,0:T(8,128)} fusion(bf16[2048,2048]{1,0:T(8,128)(2,1)} %all-gather.5.cloned.1.call-done, bf16[2048,1024]{1,0:T(8,128)(2,1)} %collective-permute-done.19), kind=kOutput, calls=%fused_computation.117 | convolution fusion | flops 8589934592 | bytes 20971520 | tf_op jit(solution)/shard_map/dot_general | solution.py:127
  305.3 16.0 %convolution_add_fusion = f32[2048,1024]{1,0:T(8,128)} fusion(f32[2048,1024]{1,0:T(8,128)} %fusion.30, bf16[2048,2048]{1,0:T(8,128)(2,1)} %all-gather.3.cloned.1.call-done, bf16[2048,1024]{1,0:T(8,128)(2,1)} %bitcast.83), kind=kOutput, calls=%fused_computation.5 | convolution fusion | flops 8592031744 | bytes 29360128 | tf_op jit(solution)/shard_map/dot_general | solution.py:125
  (73 shorter events, 6.4 us)
Async XLA Ops:
  7.2 51.9 %copy-start = (bf16[1024,1024]{1,0:T(8,128)(2,1)S(1)}, bf16[1024,1024]{1,0:T(8,128)(2,1)}, u32[]{:S(2)}) copy-start(bf16[1024,1024]{1,0:T(8,128)(2,1)} %param.9) | copy-start | bytes 6291460
  7.2 10.5 %copy-start.6 = (s32[128]{0:T(128)S(1)}, s32[128]{0:T(128)}, u32[]{:S(2)}) copy-start(s32[128]{0:T(128)} %param.13) | copy-start | bytes 1540
  7.2 283.5 %all-gather.5.cloned.1.call-start = ((), (), s32[]{:S(2)}) async-start(), calls=%async_computation.5 | async-start | bytes 8912896 | tf_op jit(solution)/shard_map/all_gather | solution.py:55
  8.7 15.2 %copy-start.2 = (bf16[128,2048]{1,0:T(8,128)(2,1)}, bf16[128,2048]{1,0:T(8,128)(2,1)S(1)}, u32[]{:S(2)}) copy-start(bf16[128,2048]{1,0:T(8,128)(2,1)S(1)} %get-tuple-element.9) | copy-start | bytes 1572868
  8.7 3.0 collective-permute-start
  11.7 0.8 copy-start.3
  17.3 2.1 collective-permute-start.1
  23.9 35.2 %all-to-all-start = ((bf16[16,48,1024]{2,1,0:T(8,128)(2,1)}), bf16[16,48,1024]{2,1,0:T(8,128)(2,1)}, u32[]{:S(2)}, u32[]{:S(2)}) async-start(bf16[16,48,1024]{2,1,0:T(8,128)(2,1)} %bitcast.81), calls=%async_computation | async-start | bytes 3145728 | tf_op jit(solution)/shard_map/all_to_all | solution.py:76
  62.3 7.7 %copy-start.5 = (s32[128,4,32]{0,2,1:T(8,128)S(1)}, s32[128,4,32]{0,2,1:T(8,128)}, u32[]{:S(2)}) copy-start(s32[128,4,32]{0,2,1:T(8,128)} %param.12) | copy-start | bytes 196612
  62.3 7.9 %copy-start.4 = (f32[128,4,32]{0,2,1:T(8,128)S(1)}, f32[128,4,32]{0,2,1:T(8,128)}, u32[]{:S(2)}) copy-start(f32[128,4,32]{0,2,1:T(8,128)} %param.10) | copy-start | bytes 196612
  64.5 19.8 %all-to-all-start.1 = ((f32[16,48,128]{2,1,0:T(8,128)}), f32[16,48,128]{2,1,0:T(8,128)S(1)}, u32[]{:S(2)}, u32[]{:S(2)}) async-start(f32[16,48,128]{2,1,0:T(8,128)} %bitcast.4), calls=%async_computation.1 | async-start | bytes 786432 | tf_op jit(solution)/shard_map/all_to_all | solution.py:85
  90.6 3.6 %collective-permute-start.2 = (f32[128,128]{0,1:T(8,128)S(1)}, f32[128,128]{0,1:T(8,128)S(1)}, u32[]{:S(2)}, u32[]{:S(2)}) collective-permute-start(f32[128,128]{0,1:T(8,128)S(1)} %copy.20), channel_id=1, source_target_pairs={{0,1},{1,0},{2,3},{3,2},{4,5},{5,4},{6,7},{7,6},{8,9},{9,8},{10,11... | collective-permute-start | bytes 196616 | tf_op jit(solution)/shard_map/ppermute | solution.py:94
  94.2 5.1 %collective-permute-start.3 = (f32[128,128]{0,1:T(8,128)S(1)}, f32[128,128]{0,1:T(8,128)S(1)}, u32[]{:S(2)}, u32[]{:S(2)}) collective-permute-start(f32[128,128]{0,1:T(8,128)S(1)} %add.181), channel_id=1, source_target_pairs={{0,2},{2,0},{1,3},{3,1},{4,6},{6,4},{5,7},{7,5},{8,10},{10,8},{9,1... | collective-permute-start | bytes 196616 | tf_op jit(solution)/shard_map/ppermute | solution.py:95
  106.9 10.7 %all-to-all-start.2 = ((bf16[16,48,128]{2,1,0:T(8,128)(2,1)}), bf16[16,48,128]{2,1,0:T(8,128)(2,1)S(1)}, u32[]{:S(2)}, u32[]{:S(2)}) async-start(bf16[16,48,128]{2,1,0:T(8,128)(2,1)} %bitcast.8), calls=%async_computation.2 | async-start | bytes 393216 | tf_op jit(solution)/shard_map/all_to_all | solution.py:107
  110.5 194.9 %all-gather.3.cloned.1.call-start = ((), (), s32[]{:S(2)}) async-start(), calls=%async_computation.4 | async-start | bytes 8912896 | tf_op jit(solution)/shard_map/all_gather | solution.py:54
  149.0 8.8 %collective-permute-start.4 = (bf16[128,1024]{1,0:T(8,128)(2,1)S(1)}, bf16[128,1024]{1,0:T(8,128)(2,1)S(1)}, u32[]{:S(2)}, u32[]{:S(2)}) collective-permute-start(bf16[128,1024]{1,0:T(8,128)(2,1)S(1)} %convolution_convert_fusion.2), channel_id=1, source_target_pairs={{0,8},{8,16},{16,24},{24,32},{32,40},{40,48},{48,56},{56,64},{64,7... | collective-permute-start | bytes 786440 | tf_op jit(solution)/shard_map/ppermute | solution.py:24
  157.7 10.5 %collective-permute-start.5 = (bf16[128,1024]{1,0:T(8,128)(2,1)S(1)}, bf16[128,1024]{1,0:T(8,128)(2,1)S(1)}, u32[]{:S(2)}, u32[]{:S(2)}) collective-permute-start(bf16[128,1024]{1,0:T(8,128)(2,1)S(1)} %collective-permute-done.4), channel_id=1, source_target_pairs={{0,8},{8,16},{16,24},{24,32},{32,40},{40,48},{48,56},{56,64},{64,7... | collective-permute-start | bytes 786440 | tf_op jit(solution)/shard_map/ppermute | solution.py:24
  157.7 13.8 %collective-permute-start.12 = (bf16[128,1024]{1,0:T(8,128)(2,1)S(1)}, bf16[128,1024]{1,0:T(8,128)(2,1)S(1)}, u32[]{:S(2)}, u32[]{:S(2)}) collective-permute-start(bf16[128,1024]{1,0:T(8,128)(2,1)S(1)} %convolution_convert_fusion.2), channel_id=1, source_target_pairs={{8,0},{16,8},{24,16},{32,24},{40,32},{48,40},{56,48},{64,56},{72,6... | collective-permute-start | bytes 786440 | tf_op jit(solution)/shard_map/ppermute | solution.py:26
  168.2 15.0 %collective-permute-start.6 = (bf16[128,1024]{1,0:T(8,128)(2,1)S(1)}, bf16[128,1024]{1,0:T(8,128)(2,1)S(1)}, u32[]{:S(2)}, u32[]{:S(2)}) collective-permute-start(bf16[128,1024]{1,0:T(8,128)(2,1)S(1)} %collective-permute-done.5), channel_id=1, source_target_pairs={{0,8},{8,16},{16,24},{24,32},{32,40},{40,48},{48,56},{56,64},{64,7... | collective-permute-start | bytes 786440 | tf_op jit(solution)/shard_map/ppermute | solution.py:24
  171.6 15.9 %collective-permute-start.13 = (bf16[128,1024]{1,0:T(8,128)(2,1)S(1)}, bf16[128,1024]{1,0:T(8,128)(2,1)S(1)}, u32[]{:S(2)}, u32[]{:S(2)}) collective-permute-start(bf16[128,1024]{1,0:T(8,128)(2,1)S(1)} %collective-permute-done.12), channel_id=1, source_target_pairs={{8,0},{16,8},{24,16},{32,24},{40,32},{48,40},{56,48},{64,56},{72,6... | collective-permute-start | bytes 786440 | tf_op jit(solution)/shard_map/ppermute | solution.py:26
  183.2 15.0 %collective-permute-start.7 = (bf16[128,1024]{1,0:T(8,128)(2,1)S(1)}, bf16[128,1024]{1,0:T(8,128)(2,1)S(1)}, u32[]{:S(2)}, u32[]{:S(2)}) collective-permute-start(bf16[128,1024]{1,0:T(8,128)(2,1)S(1)} %collective-permute-done.6), channel_id=1, source_target_pairs={{0,8},{8,16},{16,24},{24,32},{32,40},{40,48},{48,56},{56,64},{64,7... | collective-permute-start | bytes 786440 | tf_op jit(solution)/shard_map/ppermute | solution.py:24
  187.4 16.0 %collective-permute-start.14 = (bf16[128,1024]{1,0:T(8,128)(2,1)S(1)}, bf16[128,1024]{1,0:T(8,128)(2,1)S(1)}, u32[]{:S(2)}, u32[]{:S(2)}) collective-permute-start(bf16[128,1024]{1,0:T(8,128)(2,1)S(1)} %collective-permute-done.13), channel_id=1, source_target_pairs={{8,0},{16,8},{24,16},{32,24},{40,32},{48,40},{56,48},{64,56},{72,6... | collective-permute-start | bytes 786440 | tf_op jit(solution)/shard_map/ppermute | solution.py:26
  198.2 14.8 %collective-permute-start.8 = (bf16[128,1024]{1,0:T(8,128)(2,1)S(1)}, bf16[128,1024]{1,0:T(8,128)(2,1)S(1)}, u32[]{:S(2)}, u32[]{:S(2)}) collective-permute-start(bf16[128,1024]{1,0:T(8,128)(2,1)S(1)} %collective-permute-done.7), channel_id=1, source_target_pairs={{0,8},{8,16},{16,24},{24,32},{32,40},{40,48},{48,56},{56,64},{64,7... | collective-permute-start | bytes 786440 | tf_op jit(solution)/shard_map/ppermute | solution.py:24
  203.4 9.6 %collective-permute-start.15 = (bf16[128,1024]{1,0:T(8,128)(2,1)S(1)}, bf16[128,1024]{1,0:T(8,128)(2,1)S(1)}, u32[]{:S(2)}, u32[]{:S(2)}) collective-permute-start(bf16[128,1024]{1,0:T(8,128)(2,1)S(1)} %collective-permute-done.14), channel_id=1, source_target_pairs={{8,0},{16,8},{24,16},{32,24},{40,32},{48,40},{56,48},{64,56},{72,6... | collective-permute-start | bytes 786440 | tf_op jit(solution)/shard_map/ppermute | solution.py:26
  213.0 9.4 %collective-permute-start.9 = (bf16[128,1024]{1,0:T(8,128)(2,1)S(1)}, bf16[128,1024]{1,0:T(8,128)(2,1)S(1)}, u32[]{:S(2)}, u32[]{:S(2)}) collective-permute-start(bf16[128,1024]{1,0:T(8,128)(2,1)S(1)} %collective-permute-done.8), channel_id=1, source_target_pairs={{0,8},{8,16},{16,24},{24,32},{32,40},{40,48},{48,56},{56,64},{64,7... | collective-permute-start | bytes 786440 | tf_op jit(solution)/shard_map/ppermute | solution.py:24
  213.0 9.4 %collective-permute-start.16 = (bf16[128,1024]{1,0:T(8,128)(2,1)S(1)}, bf16[128,1024]{1,0:T(8,128)(2,1)S(1)}, u32[]{:S(2)}, u32[]{:S(2)}) collective-permute-start(bf16[128,1024]{1,0:T(8,128)(2,1)S(1)} %collective-permute-done.15), channel_id=1, source_target_pairs={{8,0},{16,8},{24,16},{32,24},{40,32},{48,40},{56,48},{64,56},{72,6... | collective-permute-start | bytes 786440 | tf_op jit(solution)/shard_map/ppermute | solution.py:26
  222.5 10.7 %collective-permute-start.10 = (bf16[128,1024]{1,0:T(8,128)(2,1)S(1)}, bf16[128,1024]{1,0:T(8,128)(2,1)}, u32[]{:S(2)}, u32[]{:S(2)}) collective-permute-start(bf16[128,1024]{1,0:T(8,128)(2,1)S(1)} %collective-permute-done.9), channel_id=1, source_target_pairs={{0,8},{8,16},{16,24},{24,32},{32,40},{40,48},{48,56},{56,64},{64,7... | collective-permute-start | bytes 786440 | tf_op jit(solution)/shard_map/ppermute | solution.py:24
  222.5 10.7 %collective-permute-start.17 = (bf16[128,1024]{1,0:T(8,128)(2,1)S(1)}, bf16[128,1024]{1,0:T(8,128)(2,1)S(1)}, u32[]{:S(2)}, u32[]{:S(2)}) collective-permute-start(bf16[128,1024]{1,0:T(8,128)(2,1)S(1)} %collective-permute-done.16), channel_id=1, source_target_pairs={{8,0},{16,8},{24,16},{32,24},{40,32},{48,40},{56,48},{64,56},{72,6... | collective-permute-start | bytes 786440 | tf_op jit(solution)/shard_map/ppermute | solution.py:26
  233.1 11.8 %collective-permute-start.11 = (bf16[128,1024]{1,0:T(8,128)(2,1)}, bf16[128,1024]{1,0:T(8,128)(2,1)}, u32[]{:S(2)}, u32[]{:S(2)}) collective-permute-start(bf16[128,1024]{1,0:T(8,128)(2,1)} %collective-permute-done.10), channel_id=1, source_target_pairs={{0,8},{8,16},{16,24},{24,32},{32,40},{40,48},{48,56},{56,64},{64,7... | collective-permute-start | bytes 786440 | tf_op jit(solution)/shard_map/ppermute | solution.py:24
  233.2 24.5 %collective-permute-start.18 = (bf16[128,1024]{1,0:T(8,128)(2,1)S(1)}, bf16[128,1024]{1,0:T(8,128)(2,1)S(1)}, u32[]{:S(2)}, u32[]{:S(2)}) collective-permute-start(bf16[128,1024]{1,0:T(8,128)(2,1)S(1)} %collective-permute-done.17), channel_id=1, source_target_pairs={{8,0},{16,8},{24,16},{32,24},{40,32},{48,40},{56,48},{64,56},{72,6... | collective-permute-start | bytes 786440 | tf_op jit(solution)/shard_map/ppermute | solution.py:26
  263.3 27.4 %collective-permute-start.19 = (bf16[2048,1024]{1,0:T(8,128)(2,1)}, bf16[2048,1024]{1,0:T(8,128)(2,1)}, u32[]{:S(2)}, u32[]{:S(2)}) collective-permute-start(bf16[2048,1024]{1,0:T(8,128)(2,1)} %bitcast.82), channel_id=1, source_target_pairs={{0,4},{4,0},{1,5},{5,1},{2,6},{6,2},{3,7},{7,3},{8,12},{12,8},{9,1... | collective-permute-start | bytes 12582920 | tf_op jit(solution)/shard_map/ppermute | solution.py:123
  305.3 16.0 %copy-start.1 = (bf16[1024,1024]{1,0:T(8,128)(2,1)S(1)}, bf16[1024,1024]{1,0:T(8,128)(2,1)}, u32[]{:S(2)}) copy-start(bf16[1024,1024]{1,0:T(8,128)(2,1)} %param.9) | copy-start | bytes 6291460
Sparse Core Ops, SparseCore 0:
  12.7 91.3 all-gather.4
  113.4 105.6 all-gather.2
